TPU v7x, 128 devices: a whole 4x4x4 slice. The times are simulated.
128 devices in a mesh: row: 32 (over y, x, core), col: 4 (over z).
Axes of the slice: x: 4, y: 4, z: 4, core: 2. Of those that a mesh axis runs over, the one named last changes fastest.
Arguments:
- embeddings: float32 [16384, 256], P(('col', 'row')), may hold values from -6 to 6
- levels: int32 [16384], P('row'), may hold values from 0 to 7
Outputs:
- responsibility: float32 [16384, 16384], P('row', 'col')
- availability: float32 [16384, 16384], P('row', 'col')
All inputs are finite; a program needn't handle non-finite values.
Results may differ from a plain program's by a relative error of at most 0.0003.
Values sent between devices are 32-bit elements; how exact they have to be, the bound alone decides.
No kernel may reach another device: no remote copies, remote signals or barrier semaphores. Data moves between devices by JAX's collectives and lax.ppermute only.
A program may use at most 64 MiB of HBM per device.

v0:
```python
import jax
import jax.numpy as jnp
from jax import lax
from jax.sharding import PartitionSpec as P

ITERS = 2
lowest_value = -1e30


def broadcast(shard, axis, root):
    return lax.dynamic_index_in_dim(lax.all_gather(shard, axis), root, 0, keepdims=False)


def rows_first(arrays, axis, dims):
    turned = [jnp.moveaxis(a, dim, 0) for a, dim in zip(arrays, dims)]
    both = jnp.concatenate([t.reshape(len(t), -1) for t in turned], axis=1)
    out, at, finished = (lax.all_gather(both, axis, axis=0, tiled=True), 0, [])
    for t, dim in zip(turned, dims):
        share = out[:, at : at + t[0].size].reshape(-1, *t.shape[1:])
        finished.append(jnp.moveaxis(share, 0, dim))
        at += t[0].size
    return tuple(finished)


def copy_for_each(shard, axis):
    copies = jnp.broadcast_to(shard, (lax.axis_size(axis), *shard.shape))
    return lax.all_to_all(copies, axis, split_axis=0, concat_axis=0, tiled=True)


def over_copies(shard, axis):
    return copy_for_each(shard, axis).sum(axis=0)


def packed_total(arrays, axis):
    vector, at, finished = (jnp.concatenate([a.reshape(-1) for a in arrays]), 0, [])
    subtotal = over_copies(vector, axis)
    for a in arrays:
        finished.append(subtotal[at : at + a.size].reshape(a.shape))
        at += a.size
    return tuple(finished)


def normalize(vectors):
    return vectors * lax.rsqrt(jnp.sum(vectors * vectors, axis=1, keepdims=True) + 1e-06)


def top_two(values):
    best_value = jnp.max(values, axis=1, keepdims=True)
    tie_count = jnp.sum(jnp.where(values == best_value, 1, 0), axis=1, keepdims=True)
    remainder = jnp.max(jnp.where(values < best_value, values, lowest_value), axis=1, keepdims=True)
    return (best_value, jnp.where(tie_count > 1, best_value, remainder))


def shards(embeddings, levels):
    row_count = levels.shape[0]
    n_row = lax.axis_size("row")
    n_col = lax.axis_size("col")
    row_idx = lax.axis_index("row")
    col_idx = lax.axis_index("col")
    span_rows = embeddings.shape[0]
    col_count = span_rows * n_row
    preference = 0.25 * levels.astype(jnp.float32) - 1.0
    column_block = lax.all_gather(embeddings, "row", axis=0, tiled=True)
    group_size = n_row // n_col
    offset = row_idx % group_size * row_count
    row_piece = lax.dynamic_slice_in_dim(column_block, offset, row_count, 0)
    row_block = broadcast(row_piece, "col", row_idx // group_size)
    unit_rows = normalize(row_block)
    unit_cols = normalize(column_block)
    product = lax.dot_general(
        unit_rows,
        unit_cols,
        (((1,), (1,)), ((), ())),
        precision=lax.Precision.HIGHEST,
        preferred_element_type=jnp.float32,
    )
    global_rows = row_idx * row_count + jnp.arange(row_count, dtype=jnp.int32)
    global_cols = col_idx * col_count + jnp.arange(col_count, dtype=jnp.int32)
    diagonal_mask = global_rows[:, None] == global_cols[None, :]
    similar = jnp.where(diagonal_mask, preference[:, None], product)
    responsibility = jnp.zeros_like(similar)
    availability = jnp.zeros_like(similar)
    for iteration in range(ITERS):
        combined = availability + similar
        best_value, second_value = top_two(combined)
        gathered_best, gathered_second = rows_first((best_value, second_value), "col", (1, 1))
        best_value, runner_up = top_two(gathered_best)
        second_value = jnp.maximum(runner_up, jnp.max(gathered_second, axis=1, keepdims=True))
        fresh = similar - jnp.where(combined >= best_value, second_value, best_value)
        responsibility = 0.5 * responsibility + 0.5 * fresh
        positive = jnp.sum(jnp.where(diagonal_mask, 0.0, jnp.maximum(responsibility, 0.0)), axis=0)
        diag_part = jnp.sum(jnp.where(diagonal_mask, responsibility, 0.0), axis=0)
        column_positive, self_resp = packed_total((positive, diag_part), "row")
        renewed = jnp.where(
            diagonal_mask,
            column_positive[None, :],
            jnp.minimum(
                0.0,
                self_resp[None, :] + column_positive[None, :] - jnp.maximum(responsibility, 0.0),
            ),
        )
        availability = 0.5 * availability + 0.5 * renewed
    return (responsibility, availability)


def solution(mesh):
    placed = (P(("col", "row"), None), P("row"))
    return jax.shard_map(
        shards,
        mesh=mesh,
        in_specs=placed,
        out_specs=(P("row", "col"), P("row", "col")),
        check_vma=False,
    )
```

profile of v0, /device:TPU:1, one launch (start us, length us, event | category | flops | bytes accessed | tf_op | source)
XLA Modules:
  0.0 213.9 jit_solution(4717225558266819181)
XLA Ops:
  7.2 0.0 all-gather.6.cloned.1.call-start
  7.2 0.7 all-gather.6.cloned.1.call-update
  7.9 0.0 all-gather.8.cloned.1.call-start
  8.0 51.8 %all-gather.6.cloned.1.call-done = f32[4096,256]{1,0:T(8,128)} async-done(((f32[128,256]{1,0:T(8,128)}), f32[4096,256]{1,0:T(8,128)}) %all-gather.6.cloned.1.call-update) | async-done | bytes 4194320 | tf_op jit(solution)/shard_map/all_gather | solution.py:63
  59.8 1.9 constant_dynamic-slice_fusion
  61.6 0.0 all-gather.8.cloned.1.call-update
  61.7 0.7 multiply_add_fusion.2
  62.4 2.8 %multiply_reduce_fusion = f32[4096]{0:T(1024)S(1)} fusion(f32[4096,256]{1,0:T(8,128)} %all-gather.6.cloned.1.call-done), kind=kLoop, calls=%fused_computation.24 | loop fusion | flops 2093056 | bytes 4210688 | tf_op jit(solution)/shard_map/reduce_sum | solution.py:44
  65.2 26.7 %all-gather.8.cloned.1.call-done = f32[2048,256]{1,0:T(8,128)} async-done(((f32[512,256]{1,0:T(8,128)}), f32[2048,256]{1,0:T(8,128)}) %all-gather.8.cloned.1.call-update) | async-done | bytes 2097168 | tf_op jit(solution)/shard_map/all_gather | solution.py:11
  91.9 1.2 fusion.11
  93.1 10.4 %fusion.20 = (f32[512]{0:T(512)S(1)}, f32[512,4096]{1,0:T(8,128)S(1)}) fusion(f32[4096,256]{1,0:T(8,128)} %all-gather.6.cloned.1.call-done, f32[4096]{0:T(1024)S(1)} %add_rsqrt_fusion, f32[4,512,256]{2,1,0:T(8,128)} %bitcast.36, s32[]{:T(128)S(6)} %select_n.121, f32[512]{0:T(512)S(1)} %add_rsqrt_fusion.1, f32[512]{0:T(512)S(1)} %multiply_add_fusion.2, ...), kind=kOutput, calls=%fused_computation.67 | convolution fusion | flops 6449921536 | bytes 13148164 | tf_op jit(solution)/shard_map/dot_general | solution.py:70
  103.5 0.0 copy-start
  103.5 1.0 fusion.6
  104.4 1.0 select_reduce_fusion.1
  105.5 9.1 %all-gather.1 = f32[4,1,1024]{2,1,0:T(1,128)S(1)} all-gather(f32[1,1,1024]{2,1,0:T(1,128)S(1)} %maximum_bitcast_fusion), channel_id=1, replica_groups=mesh['row'=32,'col'=4] {'col'}, dimensions={0}, use_global_device_ids=true | all-gather | bytes 20480 | tf_op jit(solution)/shard_map/all_gather | solution.py:17
  114.7 0.0 copy-done
  114.7 3.5 %fusion = (f32[4096]{0:T(1024)S(1)}, f32[4096]{0:T(1024)S(1)}) fusion(f32[512,4096]{1,0:T(8,128)S(1)} %get-tuple-element.18, f32[512]{0:T(512)S(1)} %select_maximum_fusion.1, f32[512]{0:T(512)S(1)} %get-tuple-element.8, s32[4096]{0:T(1024)S(1)} %iota_add_fusion, s32[512]{0:T(512)S(1)} %iota_add_fusion.1), kind=kLoop, calls=%fused_computation.9 | loop fusion | flops 20963328 | bytes 8443904 | tf_op jit(solution)/shard_map/reduce_sum | solution.py:91
  118.2 0.9 broadcast_in_dim.120
  119.2 27.4 %all_to_all.12 = f32[32,1,8192]{2,1,0:T(1,128)S(1)} all-to-all(f32[32,1,8192]{2,1,0:T(1,128)S(1)} %broadcast_in_dim.120), channel_id=1, replica_groups=mesh['row'=32,'col'=4] {'row'}, dimensions={0} | all-to-all | bytes 2097152 | tf_op jit(solution)/shard_map/all_to_all | solution.py:27
  146.6 0.7 reduce_sum.114
  147.3 6.0 %fusion.17 = (f32[512]{0:T(512)S(1)}, f32[512,4096]{1,0:T(8,128)S(1)}) fusion(f32[512,4096]{1,0:T(8,128)} %copy-done, f32[512]{0:T(512)S(1)} %select_maximum_fusion.1, f32[512]{0:T(512)S(1)} %get-tuple-element.8, f32[4096]{0:T(1024)S(1)} %get-tuple-element.16, f32[4096]{0:T(1024)S(1)} %get-tuple-element.15, s32[4096]{0:T(1024)S(1)} %iota_add_fusion, ...), kind=kLoop, calls=%fused_computation.64 | loop fusion | flops 25165312 | bytes 16834560 | tf_op jit(solution)/shard_map/reduce_max | solution.py:48
  153.4 0.0 slice-start
  153.4 1.0 fusion.7
  154.3 0.0 slice-start.1
  154.4 1.0 select_reduce_fusion
  155.4 9.3 %all-gather.2 = f32[4,1,1024]{2,1,0:T(1,128)S(1)} all-gather(f32[1,1,1024]{2,1,0:T(1,128)S(1)} %maximum_bitcast_fusion.1), channel_id=1, replica_groups=mesh['row'=32,'col'=4] {'col'}, dimensions={0}, use_global_device_ids=true | all-gather | bytes 20480 | tf_op jit(solution)/shard_map/all_gather | solution.py:17
  164.8 0.0 slice-done
  164.8 6.7 %fusion.2 = (f32[4096]{0:T(1024)S(1)}, f32[4096]{0:T(1024)S(1)}, f32[512,4096]{1,0:T(8,128)}) fusion(s32[4096]{0:T(1024)S(1)} %iota_add_fusion, s32[512]{0:T(512)S(1)} %iota_add_fusion.1, f32[512,4096]{1,0:T(8,128)S(1)} %bitcast.34, f32[512]{0:T(512)S(1)} %select_maximum_fusion, f32[512,4096]{1,0:T(8,128)S(1)} %get-tuple-element.12, ...), kind=kLoop, calls=%fused_computation.11 | loop fusion | flops 31449088 | bytes 25225216 | tf_op jit(solution)/shard_map/reduce_sum | solution.py:91
  171.5 0.9 broadcast_in_dim.123
  172.4 23.3 %all_to_all.13 = f32[32,1,8192]{2,1,0:T(1,128)S(1)} all-to-all(f32[32,1,8192]{2,1,0:T(1,128)S(1)} %broadcast_in_dim.123), channel_id=1, replica_groups=mesh['row'=32,'col'=4] {'row'}, dimensions={0} | all-to-all | bytes 2097152 | tf_op jit(solution)/shard_map/all_to_all | solution.py:27
  195.7 0.7 reduce_sum.119
  196.4 10.6 %fusion.5 = f32[512,4096]{1,0:T(8,128)} fusion(f32[512,4096]{1,0:T(8,128)} %get-tuple-element.10, f32[512,4096]{1,0:T(8,128)} %copy-done, f32[4096]{0:T(1024)S(1)} %get-tuple-element.14, f32[4096]{0:T(1024)S(1)} %get-tuple-element.13, f32[4096]{0:T(1024)S(1)} %get-tuple-element.16, f32[4096]{0:T(1024)S(1)} %get-tuple-element.15, ...), kind=kLoop, calls=%fused_computation.14 | loop fusion | flops 33554432 | bytes 25253888 | tf_op jit(solution)/shard_map/add | solution.py:102
  (26 shorter events, 0.2 us)
Async XLA Ops:
  7.2 52.6 %all-gather.6.cloned.1.call-start = ((), (), s32[]{:S(2)}) async-start(), calls=%async_computation.2 | async-start | bytes 4325376 | tf_op jit(solution)/shard_map/all_gather | solution.py:63
  7.9 84.0 %all-gather.8.cloned.1.call-start = ((), (), s32[]{:S(2)}) async-start(), calls=%async_computation.3 | async-start | bytes 2621440 | tf_op jit(solution)/shard_map/all_gather | solution.py:11
  103.5 11.3 %copy-start = (f32[512,4096]{1,0:T(8,128)}, f32[512,4096]{1,0:T(8,128)S(1)}, u32[]{:S(2)}) copy-start(f32[512,4096]{1,0:T(8,128)S(1)} %get-tuple-element.18) | copy-start | bytes 25165828
  153.4 11.4 %slice-start = ((s8[8388608]{0:T(1024)(128)(4,1)}), s8[4194304]{0:T(1024)(128)(4,1)S(1)}, s32[]{:S(2)}) async-start(s8[8388608]{0:T(1024)(128)(4,1)} %bitcast.33), calls=%async_computation.4 | async-start | bytes 8388608
  154.3 10.4 %slice-start.1 = ((s8[8388608]{0:T(1024)(128)(4,1)}), s8[4194304]{0:T(1024)(128)(4,1)S(1)}, s32[]{:S(2)}) async-start(s8[8388608]{0:T(1024)(128)(4,1)} %bitcast.33), calls=%async_computation.5 | async-start | bytes 8388608
Sparse Core Ops, SparseCore 0:
  10.2 49.4 all-gather.5
  62.0 29.8 all-gather.7
where the time goes:
time: 214 us
  waiting for transfers between devices  79.2 us (37%)
  blocking collectives  69.1 us (32%)
  other arithmetic  37.1 us (17%)
  between operations  14.3 us (7%)
  matrix products  10.4 us (5%)
  local copies, waits for them, and re-layouts  3.76 us (2%)
    all_gather x1, waiting for transfers between devices, shards(): column_block = lax.all_gather(embeddings, 'row', axis=0, tiled=True)  51.8 us
    all_to_all x2, blocking collectives, copy_for_each(): return lax.all_to_all(copies, axis, split_axis=0, concat_axis=0, tiled=True)  50.7 us
    all_gather x1, waiting for transfers between devices, broadcast(): lax.all_gather(shard, axis)  26.7 us
    all_gather x2, blocking collectives, rows_first(): out, at, finished = (lax.all_gather(both, axis, axis=0, tiled=True), 0, [])  18.4 us
    add x1, other arithmetic, shards(): availability = 0.5 * availability + 0.5 * renewed  10.6 us
    dot_general x1, matrix products, shards(): lax.dot_general(unit_rows, unit_cols, (((1,), (1,)), ((), ())), precision...  10.4 us
    reduce_sum x2, other arithmetic, shards(): jnp.sum(jnp.where(diagonal_mask, 0.0, jnp.maximum(responsibility, 0.0)),...  10.2 us
    reduce_max x3, other arithmetic, top_two(): best_value = jnp.max(values, axis=1, keepdims=True)  6.09 us
  transfers between devices with their start and end apart: 2, of which 2 were waited for; matrix products, arithmetic and copies ran while one was open for 2% of the time, Pallas kernels for 0%

commit v1 on v0

--- a/solution.py
+++ b/solution.py
@@ -14,7 +14,13 @@
 def rows_first(arrays, axis, dims):
     turned = [jnp.moveaxis(a, dim, 0) for a, dim in zip(arrays, dims)]
     both = jnp.concatenate([t.reshape(len(t), -1) for t in turned], axis=1)
-    out, at, finished = (lax.all_gather(both, axis, axis=0, tiled=True), 0, [])
+    out, at, finished = (
+        jnp.concatenate(
+            lax.all_to_all(jnp.stack([both] * lax.axis_size(axis)), axis, 0, 0), axis=0
+        ),
+        0,
+        [],
+    )
     for t, dim in zip(turned, dims):
         share = out[:, at : at + t[0].size].reshape(-1, *t.shape[1:])
         finished.append(jnp.moveaxis(share, 0, dim))

time: 214 us -> 206 us (0.963)
  blocking collectives: 69.1 us -> 61 us
    all_gather x2 -> x0, blocking collectives: 18.4 us -> none  [rows_first(): out, at, finished = (lax.all_gather(both, axis, axis=0, tiled=True), 0, [])]
    all_to_all x0 -> x2, blocking collectives: none -> 13.4 us  [rows_first(): lax.all_to_all(jnp.stack([both] * lax.axis_size(axis)), axis, 0, 0)]
    all_to_all x2, blocking collectives: 50.7 us -> 47.5 us  [copy_for_each(): return lax.all_to_all(copies, axis, split_axis=0, concat_axis=0, tiled=True)]
where the time goes in v1:
time: 206 us
  waiting for transfers between devices  79.2 us (38%)
  blocking collectives  61 us (30%)
  other arithmetic  37.1 us (18%)
  between operations  14.3 us (7%)
  matrix products  10.4 us (5%)
  local copies, waits for them, and re-layouts  3.78 us (2%)
    all_gather x1, waiting for transfers between devices, shards(): column_block = lax.all_gather(embeddings, 'row', axis=0, tiled=True)  51.8 us
    all_to_all x2, blocking collectives, copy_for_each(): return lax.all_to_all(copies, axis, split_axis=0, concat_axis=0, tiled=True)  47.5 us
    all_gather x1, waiting for transfers between devices, broadcast(): lax.all_gather(shard, axis)  26.7 us
    all_to_all x2, blocking collectives, rows_first(): lax.all_to_all(jnp.stack([both] * lax.axis_size(axis)), axis, 0, 0)  13.4 us
    add x1, other arithmetic, shards(): availability = 0.5 * availability + 0.5 * renewed  10.6 us
    dot_general x1, matrix products, shards(): lax.dot_general(unit_rows, unit_cols, (((1,), (1,)), ((), ())), precision...  10.4 us
    reduce_sum x2, other arithmetic, shards(): jnp.sum(jnp.where(diagonal_mask, 0.0, jnp.maximum(responsibility, 0.0)),...  10.2 us
    reduce_max x3, other arithmetic, top_two(): best_value = jnp.max(values, axis=1, keepdims=True)  6.09 us
  transfers between devices with their start and end apart: 2, of which 2 were waited for; matrix products, arithmetic and copies ran while one was open for 2% of the time, Pallas kernels for 0%

profile of v1, /device:TPU:1, one launch (start us, length us, event | category | flops | bytes accessed | tf_op | source)
XLA Modules:
  0.0 205.8 jit_solution(14031393907567653832)
XLA Ops:
  7.2 0.0 all-gather.4.cloned.1.call-start
  7.2 0.7 all-gather.4.cloned.1.call-update
  7.9 0.0 all-gather.6.cloned.1.call-start
  8.0 51.8 %all-gather.4.cloned.1.call-done = f32[4096,256]{1,0:T(8,128)} async-done(((f32[128,256]{1,0:T(8,128)}), f32[4096,256]{1,0:T(8,128)}) %all-gather.4.cloned.1.call-update) | async-done | bytes 4194320 | tf_op jit(solution)/shard_map/all_gather | solution.py:69
  59.8 1.9 constant_dynamic-slice_fusion
  61.6 0.0 all-gather.6.cloned.1.call-update
  61.7 0.7 multiply_add_fusion.2
  62.4 2.8 %multiply_reduce_fusion = f32[4096]{0:T(1024)S(1)} fusion(f32[4096,256]{1,0:T(8,128)} %all-gather.4.cloned.1.call-done), kind=kLoop, calls=%fused_computation.24 | loop fusion | flops 2093056 | bytes 4210688 | tf_op jit(solution)/shard_map/reduce_sum | solution.py:50
  65.2 26.7 %all-gather.6.cloned.1.call-done = f32[2048,256]{1,0:T(8,128)} async-done(((f32[512,256]{1,0:T(8,128)}), f32[2048,256]{1,0:T(8,128)}) %all-gather.6.cloned.1.call-update) | async-done | bytes 2097168 | tf_op jit(solution)/shard_map/all_gather | solution.py:11
  91.9 1.2 fusion.11
  93.1 10.4 %fusion.20 = (f32[512]{0:T(512)S(1)}, f32[512,4096]{1,0:T(8,128)S(1)}) fusion(f32[4096,256]{1,0:T(8,128)} %all-gather.4.cloned.1.call-done, f32[4096]{0:T(1024)S(1)} %add_rsqrt_fusion, f32[4,512,256]{2,1,0:T(8,128)} %bitcast.34, s32[]{:T(128)S(6)} %select_n.121, f32[512]{0:T(512)S(1)} %add_rsqrt_fusion.1, f32[512]{0:T(512)S(1)} %multiply_add_fusion.2, ...), kind=kOutput, calls=%fused_computation.67 | convolution fusion | flops 6449921536 | bytes 13148164 | tf_op jit(solution)/shard_map/dot_general | solution.py:76
  103.5 0.0 copy-start
  103.5 1.0 fusion.6
  104.4 1.0 select_reduce_fusion.1
  105.5 6.8 %all_to_all.22 = f32[4,1,1024]{2,1,0:T(1,128)S(1)} all-to-all(f32[4,1,1024]{2,1,0:T(1,128)S(1)} %stack.4), channel_id=1, replica_groups=mesh['row'=32,'col'=4] {'col'}, dimensions={0} | all-to-all | bytes 32768 | tf_op jit(solution)/shard_map/all_to_all | solution.py:19
  112.4 0.0 copy-done
  112.4 3.5 %fusion = (f32[4096]{0:T(1024)S(1)}, f32[4096]{0:T(1024)S(1)}) fusion(f32[512,4096]{1,0:T(8,128)S(1)} %get-tuple-element.18, f32[512]{0:T(512)S(1)} %select_maximum_fusion.1, f32[512]{0:T(512)S(1)} %get-tuple-element.8, s32[4096]{0:T(1024)S(1)} %iota_add_fusion, s32[512]{0:T(512)S(1)} %iota_add_fusion.1), kind=kLoop, calls=%fused_computation.9 | loop fusion | flops 20963328 | bytes 8443904 | tf_op jit(solution)/shard_map/reduce_sum | solution.py:97
  115.9 0.9 broadcast_in_dim.120
  116.8 26.0 %all_to_all.23 = f32[32,1,8192]{2,1,0:T(1,128)S(1)} all-to-all(f32[32,1,8192]{2,1,0:T(1,128)S(1)} %broadcast_in_dim.120), channel_id=1, replica_groups=mesh['row'=32,'col'=4] {'row'}, dimensions={0} | all-to-all | bytes 2097152 | tf_op jit(solution)/shard_map/all_to_all | solution.py:33
  142.8 0.7 reduce_sum.114
  143.5 6.0 %fusion.17 = (f32[512]{0:T(512)S(1)}, f32[512,4096]{1,0:T(8,128)S(1)}) fusion(f32[512,4096]{1,0:T(8,128)} %copy-done, f32[512]{0:T(512)S(1)} %select_maximum_fusion.1, f32[512]{0:T(512)S(1)} %get-tuple-element.8, f32[4096]{0:T(1024)S(1)} %get-tuple-element.16, f32[4096]{0:T(1024)S(1)} %get-tuple-element.15, s32[4096]{0:T(1024)S(1)} %iota_add_fusion, ...), kind=kLoop, calls=%fused_computation.64 | loop fusion | flops 25165312 | bytes 16834560 | tf_op jit(solution)/shard_map/reduce_max | solution.py:54
  149.6 0.0 slice-start
  149.6 1.0 fusion.7
  150.5 0.0 slice-start.1
  150.5 1.0 select_reduce_fusion
  151.6 6.7 %all_to_all.24 = f32[4,1,1024]{2,1,0:T(1,128)S(1)} all-to-all(f32[4,1,1024]{2,1,0:T(1,128)S(1)} %stack.5), channel_id=1, replica_groups=mesh['row'=32,'col'=4] {'col'}, dimensions={0} | all-to-all | bytes 32768 | tf_op jit(solution)/shard_map/all_to_all | solution.py:19
  158.4 0.0 slice-done
  158.4 6.7 %fusion.2 = (f32[4096]{0:T(1024)S(1)}, f32[4096]{0:T(1024)S(1)}, f32[512,4096]{1,0:T(8,128)}) fusion(s32[4096]{0:T(1024)S(1)} %iota_add_fusion, s32[512]{0:T(512)S(1)} %iota_add_fusion.1, f32[512,4096]{1,0:T(8,128)S(1)} %bitcast.32, f32[512]{0:T(512)S(1)} %select_maximum_fusion, f32[512,4096]{1,0:T(8,128)S(1)} %get-tuple-element.12, ...), kind=kLoop, calls=%fused_computation.11 | loop fusion | flops 31449088 | bytes 25225216 | tf_op jit(solution)/shard_map/reduce_sum | solution.py:97
  165.1 0.9 broadcast_in_dim.123
  166.1 21.5 %all_to_all.25 = f32[32,1,8192]{2,1,0:T(1,128)S(1)} all-to-all(f32[32,1,8192]{2,1,0:T(1,128)S(1)} %broadcast_in_dim.123), channel_id=1, replica_groups=mesh['row'=32,'col'=4] {'row'}, dimensions={0} | all-to-all | bytes 2097152 | tf_op jit(solution)/shard_map/all_to_all | solution.py:33
  187.6 0.7 reduce_sum.119
  188.3 10.6 %fusion.5 = f32[512,4096]{1,0:T(8,128)} fusion(f32[512,4096]{1,0:T(8,128)} %get-tuple-element.10, f32[512,4096]{1,0:T(8,128)} %copy-done, f32[4096]{0:T(1024)S(1)} %get-tuple-element.14, f32[4096]{0:T(1024)S(1)} %get-tuple-element.13, f32[4096]{0:T(1024)S(1)} %get-tuple-element.16, f32[4096]{0:T(1024)S(1)} %get-tuple-element.15, ...), kind=kLoop, calls=%fused_computation.14 | loop fusion | flops 33554432 | bytes 25253888 | tf_op jit(solution)/shard_map/add | solution.py:108
  (28 shorter events, 0.3 us)
Async XLA Ops:
  7.2 52.6 %all-gather.4.cloned.1.call-start = ((), (), s32[]{:S(2)}) async-start(), calls=%async_computation.4 | async-start | bytes 4325376 | tf_op jit(solution)/shard_map/all_gather | solution.py:69
  7.9 84.0 %all-gather.6.cloned.1.call-start = ((), (), s32[]{:S(2)}) async-start(), calls=%async_computation.5 | async-start | bytes 2621440 | tf_op jit(solution)/shard_map/all_gather | solution.py:11
  103.5 8.9 %copy-start = (f32[512,4096]{1,0:T(8,128)}, f32[512,4096]{1,0:T(8,128)S(1)}, u32[]{:S(2)}) copy-start(f32[512,4096]{1,0:T(8,128)S(1)} %get-tuple-element.18) | copy-start | bytes 25165828
  149.6 8.9 %slice-start = ((s8[8388608]{0:T(1024)(128)(4,1)}), s8[4194304]{0:T(1024)(128)(4,1)S(1)}, s32[]{:S(2)}) async-start(s8[8388608]{0:T(1024)(128)(4,1)} %bitcast.31), calls=%async_computation.6 | async-start | bytes 8388608
  150.5 7.9 %slice-start.1 = ((s8[8388608]{0:T(1024)(128)(4,1)}), s8[4194304]{0:T(1024)(128)(4,1)S(1)}, s32[]{:S(2)}) async-start(s8[8388608]{0:T(1024)(128)(4,1)} %bitcast.31), calls=%async_computation.7 | async-start | bytes 8388608
Sparse Core Ops, SparseCore 0:
  10.2 49.4 all-gather.3
  62.0 29.8 all-gather.5
